TPU v7x, 256 devices: a whole 4x4x8 slice. The times are simulated.
256 devices in a mesh: gx: 8 (over x, core), gy: 32 (over y, z).
Axes of the slice: x: 4, y: 4, z: 8, core: 2. Of those that a mesh axis runs over, the one named last changes fastest.
Arguments:
- fields: bfloat16 [672, 672, 1536], P('gx', 'gy'), may hold values from -16 to 16
- x_factor: bfloat16 [672, 336], replicated, may hold values from -0.00030517578 to 0.00030517578
- running_r: float32 [672, 672], replicated, as said below
Outputs:
- new_r: float32 [672, 672], P('gy', 'gx')
Inputs may be any that keep to these rules, and one draw needn't show every extreme that they name: `running_r`: upper triangular with a positive diagonal.
All inputs are finite; a program needn't handle non-finite values.
Results may differ from a plain program's by a relative error of at most 0.0003.
Values may be sent and summed in bfloat16 or wider, within the bound.
A program may use at most 256 MiB of HBM per device.

v0:
```python
import functools

import jax
import jax.numpy as jnp
from jax import lax
from jax.experimental import pallas as pl
from jax.experimental.pallas import tpu as pltpu
from jax.sharding import PartitionSpec as P

MESH = pl.DeviceIdType.MESH
LANES = 128
ROWS = 8
UNIT = 16
HIGH = lax.Precision.HIGHEST


def round_up(value, step):
    return -(-value // step) * step


class Plan:
    def __init__(self, n_gx, n_gy, x_block, y_block, cells, rank, full_y):
        self.n_gx, self.n_gy = n_gx, n_gy
        self.chips = n_gx // 2
        self.x_block = x_block
        self.x_pad = round_up(x_block, 32)
        self.y_block = y_block
        self.y_first = (y_block + 1) // 2
        self.y_common = y_block // 2
        self.cell_tiles = cells // LANES // self.chips
        self.part_cells = self.cell_tiles * LANES
        self.rank = rank
        self.rank_units = rank // UNIT
        self.units = self.cell_tiles * self.rank_units
        self.full_y = full_y
        self.y_lanes = round_up(full_y, LANES)
        self.chunks = self.make_chunks()
        tiles = []
        for row in range(0, full_y, ROWS):
            for tile in range(row // LANES, self.y_lanes // LANES):
                tiles.append((row, tile))
        self.tiles = tiles
        owners = min(n_gy, -(-len(tiles) // (2 * n_gx)))
        self.per_owner = -(-len(tiles) // (n_gx * owners))
        self.owners = -(-len(tiles) // (n_gx * self.per_owner))
        self.piece = self.per_owner * self.owners
        self.half = self.piece * self.chips
        self.n_tiles = 2 * self.half

    def make_chunks(self):
        count = min(5, self.y_common)
        bounds = [self.y_common * i // count for i in range(count + 1)]
        return [(low, high - low) for low, high in zip(bounds[:-1], bounds[1:])]


def exchange_kernel(
    plan, f_hbm, xt_ref, r_ref, out_ref,
    fbuf, fibres, pbuf, gbuf, mbuf, gram, tiles, summed, core_in, x_in, y_in,
    s1_send, s1_recv, s2_send, s2_recv, e_send, e_recv, rs_send, rs_recv, loc,
):
    n_gx, n_gy, chips = plan.n_gx, plan.n_gy, plan.chips
    gx = lax.axis_index("gx")
    gy = lax.axis_index("gy")
    xi = gx // 2
    core = gx % 2
    units = plan.units
    has_extra = plan.y_first > plan.y_common
    extra_slot = len(plan.chunks)

    def remote(src, dst, send, recv, to_gx, to_gy):
        return pltpu.make_async_remote_copy(
            src_ref=src, dst_ref=dst, send_sem=send, recv_sem=recv,
            device_id=(to_gx, to_gy), device_id_type=MESH,
        )

    barrier = pltpu.get_barrier_semaphore()

    @pl.loop(1, n_gx)
    def _(step):
        pl.semaphore_signal(barrier, inc=1, device_id=(lax.rem(gx + step, n_gx), gy), device_id_type=MESH)

    @pl.loop(1, n_gy)
    def _(step):
        to_gy = lax.rem(gy + step, n_gy)
        pl.semaphore_signal(barrier, inc=1, device_id=(2 * xi, to_gy), device_id_type=MESH)
        pl.semaphore_signal(barrier, inc=1, device_id=(2 * xi + 1, to_gy), device_id_type=MESH)

    if plan.x_pad > plan.x_block:
        for block in range(n_gx):
            low = block * plan.x_pad + plan.x_block
            high = (block + 1) * plan.x_pad
            fibres[low:high, :] = jnp.zeros((high - low, plan.part_cells), jnp.bfloat16)

    pl.semaphore_wait(barrier, (n_gx - 1) + 2 * (n_gy - 1))

    def field_src(to_core, to_chip, low, size):
        return f_hbm.at[
            pl.ds(plan.y_first * to_core + low, size), :,
            pl.ds(pl.multiple_of(plan.part_cells * to_chip, LANES), plan.part_cells),
        ]

    def field_dst(low, size):
        return fbuf.at[pl.ds(low, size), gx]

    def stage1(index, low, size):
        local = pltpu.make_async_copy(
            field_src(core, xi, low, size), field_dst(low, size), s1_recv.at[index, gx]
        )
        local.start()

        @pl.loop(1, n_gx)
        def _(step):
            to = lax.rem(gx + step, n_gx)
            remote(
                field_src(to % 2, to // 2, low, size), field_dst(low, size),
                s1_send.at[index], s1_recv.at[index, gx], to, gy,
            ).start()

    for index, (low, size) in enumerate(plan.chunks):
        stage1(index, low, size)
    low_extra = plan.y_common
    if has_extra:
        @pl.loop(1, chips)
        def _(step):
            to_chip = lax.rem(xi + step, chips)
            remote(
                field_src(0, to_chip, low_extra, 1), field_dst(low_extra, 1),
                s1_send.at[extra_slot], s1_recv.at[extra_slot, gx], 2 * to_chip, gy,
            ).start()

        @pl.when(core == 0)
        def _():
            pltpu.make_async_copy(
                field_src(0, xi, low_extra, 1), field_dst(low_extra, 1), s1_recv.at[extra_slot, gx]
            ).start()

        @pl.when(core == 1)
        def _():
            remote(
                field_src(0, xi, low_extra, 1), field_dst(low_extra, 1),
                s1_send.at[extra_slot], s1_recv.at[extra_slot, gx], 2 * xi, gy,
            ).start()

    def project(y):
        for block in range(n_gx):
            low = block * plan.x_pad
            fibres[low:low + plan.x_block, :] = fbuf[y, block]
        product = jnp.dot(xt_ref[...], fibres[...], preferred_element_type=jnp.float32).astype(jnp.bfloat16)
        for tile in range(plan.cell_tiles):
            part = product[:, tile * LANES:(tile + 1) * LANES]
            pbuf[y, pl.ds(tile * plan.rank_units, plan.rank_units)] = part.reshape(plan.rank_units, UNIT, LANES)

    def tile_src(unit, low, size):
        return pbuf.at[pl.ds(low, size), lax.rem(unit, units)]

    def tile_dst(low, size):
        return gbuf.at[pl.ds(plan.y_block * gy + plan.y_first * core + low, size)]

    def stage2(low, size, send, recv):
        pltpu.make_async_copy(tile_src(2 * gy + core, low, size), tile_dst(low, size), recv).start()
        remote(
            tile_src(2 * gy + 1 - core, low, size), tile_dst(low, size), send, recv, 2 * xi + 1 - core, gy
        ).start()

        @pl.loop(1, n_gy)
        def _(step):
            to_gy = lax.rem(gy + step, n_gy)
            for to_core in range(2):
                remote(
                    tile_src(2 * to_gy + to_core, low, size), tile_dst(low, size), send, recv,
                    2 * xi + to_core, to_gy,
                ).start()

    def chunk_done(index, low, size):
        for source in range(n_gx):
            there = fbuf.at[pl.ds(low, size), source]
            pltpu.make_async_copy(there, there, s1_recv.at[index, source]).wait()

    for index, (low, size) in enumerate(plan.chunks):
        chunk_done(index, low, size)

        @pl.loop(low, low + size)
        def _(y):
            project(y)

        stage2(low, size, s2_send, s2_recv)

    if has_extra:
        @pl.when(core == 0)
        def _():
            chunk_done(extra_slot, low_extra, 1)
            project(low_extra)
            stage2(low_extra, 1, e_send, s2_recv)

    n_y = plan.full_y
    for low in range(0, n_y, LANES):
        high = min(low + LANES, n_y)
        out_ref[low:high, low:n_y] = lax.dot_general(
            r_ref[0:high, low:high], r_ref[0:high, low:n_y], (((0,), (0,)), ((), ())),
            precision=HIGH, preferred_element_type=jnp.float32,
        )
        if low:
            out_ref[low:high, 0:low] = jnp.zeros((high - low, low), jnp.float32)

    size = UNIT * UNIT
    to_row = lax.broadcasted_iota(jnp.int32, (size, size), 0)
    from_row = lax.broadcasted_iota(jnp.int32, (size, size), 1)
    turn = ((to_row % UNIT == from_row // UNIT) & (to_row // UNIT == from_row % UNIT)).astype(jnp.bfloat16)

    pltpu.make_async_copy(gbuf, gbuf, s2_recv).wait()

    @pl.loop(0, n_y // UNIT)
    def _(group):
        rows = pl.ds(pl.multiple_of(group * UNIT, UNIT), UNIT)
        block = gbuf[rows].reshape(size, LANES)
        turned = jnp.dot(turn, block, preferred_element_type=jnp.float32).astype(jnp.bfloat16)
        turned = turned.reshape(UNIT, UNIT, LANES)
        for a in range(UNIT):
            mbuf[a // 2, rows, (a % 2) * LANES:(a % 2 + 1) * LANES] = turned[a]

    keep = jnp.where(2 * gy + core < units, 1.0, 0.0).astype(jnp.float32)
    for low in range(0, n_y, LANES):
        high = min(low + LANES, n_y)
        total = jnp.zeros((high - low, n_y - low), jnp.float32)
        for a in range(UNIT // 2):
            total = total + lax.dot_general(
                mbuf[a, low:high, :], mbuf[a, low:n_y, :], (((1,), (1,)), ((), ())),
                preferred_element_type=jnp.float32,
            )
        gram[low:high, low:n_y] = total * keep

    gap = plan.y_lanes - n_y
    for index, (row, tile) in enumerate(plan.tiles):
        width = min(LANES, n_y - tile * LANES)
        if width < LANES:
            tiles[index] = jnp.zeros((ROWS, LANES), jnp.float32)
        tiles[index, :, 0:width] = gram[row:row + ROWS, tile * LANES:tile * LANES + width]
    for index in range(len(plan.tiles), plan.n_tiles):
        tiles[index] = jnp.zeros((ROWS, LANES), jnp.float32)

    half, piece, own = plan.half, plan.piece, plan.per_owner
    my_half = core * half
    other_half = (1 - core) * half
    send = remote(
        tiles.at[pl.ds(other_half, half)], core_in, rs_send.at[0], rs_recv.at[0], 2 * xi + 1 - core, gy
    )
    send.start()
    send.wait()

    def add_core(i):
        tiles[my_half + i] += core_in[i]
    pl.loop(0, half)(add_core)

    x_sends = []
    for step in range(1, chips):
        to = lax.rem(xi + step, chips)
        send = remote(
            tiles.at[pl.ds(my_half + to * piece, piece)], x_in.at[step], rs_send.at[1], rs_recv.at[step],
            2 * to + core, gy,
        )
        send.start()
        x_sends.append(send)
    for send in x_sends:
        send.wait_recv()
    my_piece = my_half + xi * piece

    def add_x(i):
        value = tiles[my_piece + i]
        for step in range(1, chips):
            value = value + x_in[step, i]
        tiles[my_piece + i] = value
    pl.loop(0, piece)(add_x)

    @pl.loop(1, n_gy)
    def _(step):
        to = lax.rem(gy + step, n_gy)

        @pl.when(to < plan.owners)
        def _():
            remote(
                tiles.at[pl.ds(my_piece + to * own, own)], y_in.at[pl.ds(gy * own, own)], rs_send.at[2], rs_recv.at[chips],
                gx, to,
            ).start()

    @pl.when(gy < plan.owners)
    def _():
        mine = my_piece + gy * own
        pltpu.make_async_copy(
            tiles.at[pl.ds(mine, own)], y_in.at[pl.ds(gy * own, own)], rs_recv.at[chips]
        ).start()
        pltpu.make_async_copy(y_in, y_in, rs_recv.at[chips]).wait()
        for i in range(own):
            value = y_in[i]
            for source in range(1, n_gy):
                value = value + y_in[source * own + i]
            summed[mine + i] = value

        @pl.loop(1, n_gy)
        def _(step):
            to = lax.rem(gy + step, n_gy)
            remote(
                summed.at[pl.ds(mine, own)], summed.at[pl.ds(mine, own)], rs_send.at[3], e_recv.at[0], gx, to
            ).start()

    sent_own = tiles.at[pl.ds(my_piece, own)]

    @pl.loop(1, n_gy)
    def _(step):
        to = lax.rem(gy + step, n_gy)

        @pl.when(to < plan.owners)
        def _():
            pltpu.make_async_copy(sent_own, sent_own, rs_send.at[2]).wait()

    whole = summed.at[pl.ds(my_piece, piece)]
    rest = summed.at[pl.ds(my_piece, piece - own)]

    @pl.when(gy < plan.owners)
    def _():
        if plan.owners > 1:
            pltpu.make_async_copy(rest, rest, e_recv.at[0]).wait()

    @pl.when(gy >= plan.owners)
    def _():
        pltpu.make_async_copy(whole, whole, e_recv.at[0]).wait()

    gathers = []
    for step in range(1, chips):
        to = lax.rem(xi + step, chips)
        send = remote(whole, whole, rs_send.at[4], e_recv.at[step], 2 * to + core, gy)
        send.start()
        gathers.append(send)
    for send in gathers:
        send.wait_recv()
    mine_half = summed.at[pl.ds(my_half, half)]
    last = remote(mine_half, mine_half, rs_send.at[5], e_recv.at[chips], 2 * xi + 1 - core, gy)
    last.start()
    last.wait()

    for index, (row, tile) in enumerate(plan.tiles):
        width = min(LANES, n_y - tile * LANES)
        where = (slice(row, row + ROWS), slice(tile * LANES, tile * LANES + width))
        out_ref[where] = out_ref[where] + summed[index, :, 0:width]

    for send in x_sends:
        send.wait_send()
    for send in gathers:
        send.wait_send()

    @pl.when(gy < plan.owners)
    def _():
        @pl.loop(1, n_gy)
        def _(step):
            own_tiles = y_in.at[pl.ds(0, own)]
            pltpu.make_async_copy(own_tiles, own_tiles, rs_send.at[3]).wait()

    for index, (low, size) in enumerate(plan.chunks):
        there = fbuf.at[pl.ds(low, size), 0]

        @pl.loop(1, n_gx)
        def _(step):
            pltpu.make_async_copy(there, there, s1_send.at[index]).wait()

        tile_there = pbuf.at[pl.ds(low, size), 0]

        @pl.loop(1, 2 * n_gy)
        def _(step):
            pltpu.make_async_copy(tile_there, tile_there, s2_send).wait()
    if has_extra:
        there_extra = fbuf.at[pl.ds(low_extra, 1), 0]
        tile_extra = pbuf.at[pl.ds(low_extra, 1), 0]

        @pl.loop(1, chips)
        def _(step):
            pltpu.make_async_copy(there_extra, there_extra, s1_send.at[extra_slot]).wait()

        @pl.when(core == 1)
        def _():
            pltpu.make_async_copy(there_extra, there_extra, s1_send.at[extra_slot]).wait()

        @pl.when(core == 0)
        def _():
            @pl.loop(1, 2 * n_gy)
            def _(step):
                pltpu.make_async_copy(tile_extra, tile_extra, e_send).wait()


def updated_total(plan, fields, x_factor, running_r):
    by_y = jnp.transpose(fields, (1, 0, 2))
    xt = jnp.transpose(x_factor).reshape(plan.rank, plan.n_gx, plan.x_block)
    xt = jnp.pad(xt, ((0, 0), (0, 0), (0, plan.x_pad - plan.x_block))).reshape(plan.rank, plan.n_gx * plan.x_pad)
    n_y = plan.full_y
    chunks = len(plan.chunks) + 1
    vmem = pl.BlockSpec(memory_space=pltpu.VMEM)
    return pl.pallas_call(
        functools.partial(exchange_kernel, plan),
        out_shape=jax.ShapeDtypeStruct((n_y, n_y), jnp.float32),
        in_specs=[pl.BlockSpec(memory_space=pl.ANY), vmem, vmem],
        out_specs=vmem,
        scratch_shapes=[
            pltpu.VMEM((plan.y_first, plan.n_gx, plan.x_block, plan.part_cells), jnp.bfloat16),
            pltpu.VMEM((plan.n_gx * plan.x_pad, plan.part_cells), jnp.bfloat16),
            pltpu.VMEM((plan.y_first, plan.units, UNIT, LANES), jnp.bfloat16),
            pltpu.VMEM((n_y, UNIT, LANES), jnp.bfloat16),
            pltpu.VMEM((UNIT // 2, n_y, 2 * LANES), jnp.bfloat16),
            pltpu.VMEM((n_y, n_y), jnp.float32),
            pltpu.VMEM((plan.n_tiles, ROWS, LANES), jnp.float32),
            pltpu.VMEM((plan.n_tiles, ROWS, LANES), jnp.float32),
            pltpu.VMEM((plan.half, ROWS, LANES), jnp.float32),
            pltpu.VMEM((plan.chips, plan.piece, ROWS, LANES), jnp.float32),
            pltpu.VMEM((plan.n_gy * plan.per_owner, ROWS, LANES), jnp.float32),
            pltpu.SemaphoreType.DMA((chunks,)),
            pltpu.SemaphoreType.DMA((chunks, plan.n_gx)),
            pltpu.SemaphoreType.DMA,
            pltpu.SemaphoreType.DMA,
            pltpu.SemaphoreType.DMA,
            pltpu.SemaphoreType.DMA((plan.chips + 1,)),
            pltpu.SemaphoreType.DMA((6,)),
            pltpu.SemaphoreType.DMA((plan.chips + 1,)),
            pltpu.SemaphoreType.DMA,
        ],
        compiler_params=pltpu.CompilerParams(
            collective_id=0, has_side_effects=True, vmem_limit_bytes=48 * 1024 * 1024
        ),
        name="exchange",
    )(by_y, xt, running_r)


def element(row, lane):
    return jnp.broadcast_to(row[0:1, lane:lane + 1], (ROWS, LANES))

def factor_panel(rows, lane):
    rows = list(rows)
    diag = {(k, i): element(rows[k], lane + i) for k in range(ROWS) for i in range(k, ROWS)}
    done = []
    for k in range(ROWS):
        inv = lax.rsqrt(diag[k, k])
        scaled = {i: diag[k, i] * inv for i in range(k + 1, ROWS)}
        top = rows[k] * inv
        done.append(top)
        for i in range(k + 1, ROWS):
            for j in range(i, ROWS):
                diag[i, j] = diag[i, j] - scaled[i] * scaled[j]
            rows[i] = rows[i] - scaled[i] * top
    return done

def chol_kernel(n, a_ref, u_ref, work, rowbuf, spread):
    nb = -(-n // LANES); width = nb * LANES
    for t in range(nb):
        w = min(LANES, n - t * LANES)
        work[t, 0:n, 0:w] = a_ref[:, t * LANES:t * LANES + w]

    def block(b, panels, tiles):
        start = pl.multiple_of(b * LANES, LANES)
        for p in range(panels):
            for s in range(tiles):
                t = jnp.minimum(b + s, nb - 1)
                rowbuf[pl.ds(p * 64 + s, ROWS, stride=ROWS), :] = work[t, pl.ds(start + p * ROWS, ROWS), :]
        def get(i):
            return rowbuf[i * ROWS:(i + 1) * ROWS, :]
        def put(i, v):
            rowbuf[i * ROWS:(i + 1) * ROWS, :] = v
        rows = [get(i) for i in range(ROWS)]
        for p in range(panels):
            lane = p * ROWS
            done = factor_panel(rows, lane)
            for k in range(ROWS):
                put(lane + k, done[k])
            if p + 1 == panels:
                break
            rows = []
            for i in range(ROWS):
                value = get(lane + ROWS + i)
                acc = None
                for k in range(ROWS):
                    term = element(done[k], lane + ROWS + i) * done[k]
                    acc = term if acc is None else acc + term
                rows.append(value - acc)
            if p + 2 < panels:
                flat = rowbuf[pl.ds(lane * ROWS, ROWS, stride=ROWS), :]
                for i in range((p + 2) * ROWS, panels * ROWS):
                    spread[i * ROWS:(i + 1) * ROWS, :] = jnp.broadcast_to(flat[:, i:i + 1], (ROWS, LANES))
                    acc = None
                    for k in range(ROWS):
                        term = spread[pl.ds(i * ROWS + k, ROWS, stride=0), :] * done[k]
                        acc = term if acc is None else acc + term
                    put(i, get(i) - acc)
        for p in range(panels):
            for s in range(tiles):
                t = jnp.minimum(b + s, nb - 1)
                def move():
                    work[t, pl.ds(start + p * ROWS, ROWS), :] = rowbuf[pl.ds(p * 64 + s, ROWS, stride=ROWS), :]
                pl.when(b + s < nb)(move)

    full = n // LANES
    rest = (n - full * LANES) // ROWS
    @pl.loop(0, full)
    def _(b):
        block(b, LANES // ROWS, nb)
        for static in range(full):
            if (static + 1) * LANES < n:
                @pl.when(b == static)
                def _():
                    low = static * LANES
                    for r in range(static + 1, nb):
                        hi = min((r + 1) * LANES, n)
                        left = work[r, low:low + LANES, 0:hi - r * LANES]
                        for c in range(r, nb):
                            right = work[c, low:low + LANES, :]
                            work[c, r * LANES:hi, :] -= lax.dot_general(left, right, (((0,), (0,)), ((), ())), precision=HIGH, preferred_element_type=jnp.float32)
    if rest:
        block(full, rest, 1)
    for t in range(nb):
        w = min(LANES, n - t * LANES)
        for r in range(nb):
            hi = min((r + 1) * LANES, n); lo = r * LANES
            if r < t:
                u_ref[lo:hi, t * LANES:t * LANES + w] = work[t, lo:hi, 0:w]
            elif r > t:
                u_ref[lo:hi, t * LANES:t * LANES + w] = jnp.zeros((hi - lo, w), jnp.float32)
            else:
                v = work[t, lo:hi, 0:w]
                keep = lax.broadcasted_iota(jnp.int32, v.shape, 0) <= lax.broadcasted_iota(jnp.int32, v.shape, 1)
                u_ref[lo:hi, t * LANES:t * LANES + w] = jnp.where(keep, v, 0.0)

def upper_factor(a):
    n = a.shape[0]; nb = -(-n // LANES)
    return pl.pallas_call(
        functools.partial(chol_kernel, n),
        out_shape=jax.ShapeDtypeStruct((n, n), jnp.float32),
        in_specs=[pl.BlockSpec(memory_space=pltpu.VMEM)], out_specs=pl.BlockSpec(memory_space=pltpu.VMEM),
        scratch_shapes=[pltpu.VMEM((nb, nb * LANES, LANES), jnp.float32), pltpu.VMEM((LANES * ROWS, LANES), jnp.float32), pltpu.VMEM((LANES * ROWS, LANES), jnp.float32)],
        compiler_params=pltpu.CompilerParams(vmem_limit_bytes=40 * 1024 * 1024), name="factor",
    )(a)


def on_device(n_gx, n_gy, fields, x_factor, running_r):
    x_block, y_block, cells = fields.shape
    full_y = running_r.shape[0]
    plan = Plan(n_gx, n_gy, x_block, y_block, cells, x_factor.shape[1], full_y)
    total = updated_total(plan, fields, x_factor, running_r)
    upper_r = upper_factor(total)
    row_block = full_y // n_gy
    col_block = full_y // n_gx
    return lax.dynamic_slice(
        upper_r,
        (lax.axis_index("gy") * row_block, lax.axis_index("gx") * col_block),
        (row_block, col_block),
    )


def solution(mesh):
    in_specs = (P("gx", "gy", None), P(), P())
    out_specs = P("gy", "gx")
    return jax.shard_map(
        functools.partial(on_device, mesh.shape["gx"], mesh.shape["gy"]),
        mesh=mesh, in_specs=in_specs, out_specs=out_specs, check_vma=False,
    )
```

profile of v0, /device:TPU:1, one launch (start us, length us, event | category | flops | bytes accessed | tf_op | source)
XLA Modules:
  0.0 183.3 jit_solution(2421450542041531610)
XLA Ops:
  0.0 0.0 copy-start
  0.0 1.3 reshape.6
  1.3 0.1 pad.4
  1.4 0.2 copy.5.xt_ref
  1.6 0.1 copy-done
  1.7 144.3 %exchange.1.a_ref = f32[672,672]{1,0:T(8,128)S(1)} custom-call(bf16[21,84,1536]{2,1,0:T(8,128)(2,1)} %bitcast.5, bf16[336,768]{1,0:T(8,128)(2,1)S(1)} %copy.5.xt_ref, f32[672,672]{1,0:T(8,128)S(1)} %copy-done), custom_call_target="tpu_custom_call" | custom-call | tf_op jit(solution)/shard_map/exchange/pallas_call | solution.py:395
  146.0 36.6 %factor.1 = f32[672,672]{1,0:T(8,128)S(1)} custom-call(f32[672,672]{1,0:T(8,128)S(1)} %exchange.1.a_ref), custom_call_target="tpu_custom_call" | custom-call | tf_op jit(solution)/shard_map/factor/pallas_call | solution.py:528
  182.6 0.7 dynamic_slice.3
Async XLA Ops:
  0.0 1.7 copy-start
where the time goes:
time: 183 us
  Pallas kernels  181 us (99%)
  local copies, waits for them, and re-layouts  2.4 us (1%)
    pallas_call x1, Pallas kernels, updated_total(): pl.pallas_call(functools.partial(exchange_kernel, plan), out_shape=jax.Sh...  144 us
    pallas_call x1, Pallas kernels, upper_factor(): pl.pallas_call(functools.partial(chol_kernel, n), out_shape=jax.ShapeDtyp...  36.6 us

commit v1 on v0

--- a/solution.py
+++ b/solution.py
@@ -11,17 +11,33 @@
 LANES = 128
 ROWS = 8
 UNIT = 16
+NARROW = 32
 HIGH = lax.Precision.HIGHEST
 
 
 def round_up(value, step):
     return -(-value // step) * step
+
+
+def ring_offsets(size, distance):
+    if distance >= size:
+        return []
+    return [distance] if 2 * distance == size else [distance, size - distance]
+
+
+def doublings(size):
+    distance = 1
+    while distance < size:
+        yield distance
+        distance *= 2
 
 
 class Plan:
     def __init__(self, n_gx, n_gy, x_block, y_block, cells, rank, full_y):
         self.n_gx, self.n_gy = n_gx, n_gy
         self.chips = n_gx // 2
+        self.n_z = 8 if n_gy % 8 == 0 else n_gy
+        self.n_yy = n_gy // self.n_z
         self.x_block = x_block
         self.x_pad = round_up(x_block, 32)
         self.y_block = y_block
@@ -33,30 +49,48 @@
         self.rank_units = rank // UNIT
         self.units = self.cell_tiles * self.rank_units
         self.full_y = full_y
-        self.y_lanes = round_up(full_y, LANES)
         self.chunks = self.make_chunks()
-        tiles = []
-        for row in range(0, full_y, ROWS):
-            for tile in range(row // LANES, self.y_lanes // LANES):
-                tiles.append((row, tile))
-        self.tiles = tiles
-        owners = min(n_gy, -(-len(tiles) // (2 * n_gx)))
-        self.per_owner = -(-len(tiles) // (n_gx * owners))
-        self.owners = -(-len(tiles) // (n_gx * self.per_owner))
-        self.piece = self.per_owner * self.owners
-        self.half = self.piece * self.chips
+        self.pieces, used = self.pack()
+        self.slots = self.n_z // 2
+        self.per_owner = -(-used // (n_gx * n_gy))
+        self.part = self.chips * self.n_yy * self.slots * self.per_owner
+        self.half = 2 * self.part
         self.n_tiles = 2 * self.half
 
+    def pack(self):
+        pieces, narrow, used = [], [], 0
+        for row in range(0, self.full_y, ROWS):
+            for start in range(row // LANES * LANES, self.full_y, LANES):
+                low = max(row, start) // NARROW * NARROW
+                high = min(start + LANES, self.full_y)
+                if high - low <= NARROW:
+                    narrow.append((row, low, high - low))
+                else:
+                    pieces.append((row, start, high - start, used, 0))
+                    used += 1
+        for index, (row, low, width) in enumerate(narrow):
+            share = LANES // NARROW
+            pieces.append((row, low, width, used + index // share, index % share * NARROW))
+        return pieces, used + -(-len(narrow) * NARROW // LANES)
+
     def make_chunks(self):
-        count = min(5, self.y_common)
-        bounds = [self.y_common * i // count for i in range(count + 1)]
-        return [(low, high - low) for low, high in zip(bounds[:-1], bounds[1:])]
+        sizes = []
+        left = self.y_common
+        while left:
+            size = 1 if len(sizes) < 2 else 2
+            sizes.append(min(size, left))
+            left -= sizes[-1]
+        chunks, low = [], 0
+        for size in sizes:
+            chunks.append((low, size))
+            low += size
+        return chunks
 
 
 def exchange_kernel(
-    plan, f_hbm, xt_ref, r_ref, out_ref,
-    fbuf, fibres, pbuf, gbuf, mbuf, gram, tiles, summed, core_in, x_in, y_in,
-    s1_send, s1_recv, s2_send, s2_recv, e_send, e_recv, rs_send, rs_recv, loc,
+    plan, f_hbm, x_hbm, r_hbm, out_ref,
+    fbuf, fibres, x_rows, x_pad, xt_ref, r_ref, pbuf, gbuf, mbuf, gram, tiles, summed, core_in, axis_in, z_in,
+    s1_send, s1_recv, s2_send, s2_recv, e_send, rs_send, rs_recv, loc, hands,
 ):
     n_gx, n_gy, chips = plan.n_gx, plan.n_gy, plan.chips
     gx = lax.axis_index("gx")
@@ -73,17 +107,21 @@
             device_id=(to_gx, to_gy), device_id_type=MESH,
         )
 
+    def other_gy(step_y, step_z):
+        n_z, n_yy = plan.n_z, plan.n_yy
+        return n_z * lax.rem(gy // n_z + step_y, n_yy) + lax.rem(gy % n_z + step_z, n_z)
+
     barrier = pltpu.get_barrier_semaphore()
-
-    @pl.loop(1, n_gx)
-    def _(step):
+    near = [other_gy(0, step) for step in ring_offsets(plan.n_z, 1)]
+    near += [other_gy(step, 0) for step in ring_offsets(plan.n_yy, 1)]
+    for to_gy in near:
+        pl.semaphore_signal(barrier, inc=1, device_id=(gx, to_gy), device_id_type=MESH)
+    for step in range(1, n_gx):
         pl.semaphore_signal(barrier, inc=1, device_id=(lax.rem(gx + step, n_gx), gy), device_id_type=MESH)
-
-    @pl.loop(1, n_gy)
-    def _(step):
-        to_gy = lax.rem(gy + step, n_gy)
-        pl.semaphore_signal(barrier, inc=1, device_id=(2 * xi, to_gy), device_id_type=MESH)
-        pl.semaphore_signal(barrier, inc=1, device_id=(2 * xi + 1, to_gy), device_id_type=MESH)
+    fetch_x = pltpu.make_async_copy(x_hbm, x_rows, loc.at[0])
+    fetch_x.start()
+    fetch_r = pltpu.make_async_copy(r_hbm, r_ref, loc.at[1])
+    fetch_r.start()
 
     if plan.x_pad > plan.x_block:
         for block in range(n_gx):
@@ -91,7 +129,7 @@
             high = (block + 1) * plan.x_pad
             fibres[low:high, :] = jnp.zeros((high - low, plan.part_cells), jnp.bfloat16)
 
-    pl.semaphore_wait(barrier, (n_gx - 1) + 2 * (n_gy - 1))
+    pl.semaphore_wait(barrier, (n_gx - 1) + len(near))
 
     def field_src(to_core, to_chip, low, size):
         return f_hbm.at[
@@ -116,8 +154,6 @@
                 s1_send.at[index], s1_recv.at[index, gx], to, gy,
             ).start()
 
-    for index, (low, size) in enumerate(plan.chunks):
-        stage1(index, low, size)
     low_extra = plan.y_common
     if has_extra:
         @pl.loop(1, chips)
@@ -140,6 +176,42 @@
                 field_src(0, xi, low_extra, 1), field_dst(low_extra, 1),
                 s1_send.at[extra_slot], s1_recv.at[extra_slot, gx], 2 * xi, gy,
             ).start()
+    for index, (low, size) in enumerate(plan.chunks):
+        stage1(index, low, size)
+
+    rounds = [(0, distance) for distance in doublings(plan.n_z)] + [(distance, 0) for distance in doublings(plan.n_yy)]
+    for index, (step_y, step_z) in enumerate(rounds):
+        steps = ring_offsets(plan.n_z, step_z) if step_z else ring_offsets(plan.n_yy, step_y)
+        for step in steps:
+            to_gy = other_gy(0, step) if step_z else other_gy(step, 0)
+            pl.semaphore_signal(hands.at[index], inc=1, device_id=(gx, to_gy), device_id_type=MESH)
+        pl.semaphore_wait(hands.at[index], len(steps))
+
+    fetch_x.wait()
+    x_pad[...] = jnp.zeros_like(x_pad)
+    for block in range(n_gx):
+        x_pad[block * plan.x_pad:block * plan.x_pad + plan.x_block, :] = x_rows[
+            block * plan.x_block:(block + 1) * plan.x_block, :
+        ]
+    unit_row = lax.broadcasted_iota(jnp.int32, (plan.rank, plan.rank), 0)
+    unit_col = lax.broadcasted_iota(jnp.int32, (plan.rank, plan.rank), 1)
+    xt_ref[...] = lax.dot_general(
+        (unit_row == unit_col).astype(jnp.bfloat16), x_pad[...], (((1,), (1,)), ((), ())),
+        preferred_element_type=jnp.float32,
+    ).astype(jnp.bfloat16)
+
+    n_y = plan.full_y
+
+    def square_r():
+        fetch_r.wait()
+        for low in range(0, n_y, LANES):
+            high = min(low + LANES, n_y)
+            out_ref[low:high, low:n_y] = lax.dot_general(
+                r_ref[0:high, low:high], r_ref[0:high, low:n_y], (((0,), (0,)), ((), ())),
+                precision=HIGH, preferred_element_type=jnp.float32,
+            )
+            if low:
+                out_ref[low:high, 0:low] = jnp.zeros((high - low, low), jnp.float32)
 
     def project(y):
         for block in range(n_gx):
@@ -164,7 +236,7 @@
 
         @pl.loop(1, n_gy)
         def _(step):
-            to_gy = lax.rem(gy + step, n_gy)
+            to_gy = other_gy(step + step // plan.n_z, 3 * step)
             for to_core in range(2):
                 remote(
                     tile_src(2 * to_gy + to_core, low, size), tile_dst(low, size), send, recv,
@@ -175,15 +247,6 @@
         for source in range(n_gx):
             there = fbuf.at[pl.ds(low, size), source]
             pltpu.make_async_copy(there, there, s1_recv.at[index, source]).wait()
-
-    for index, (low, size) in enumerate(plan.chunks):
-        chunk_done(index, low, size)
-
-        @pl.loop(low, low + size)
-        def _(y):
-            project(y)
-
-        stage2(low, size, s2_send, s2_recv)
 
     if has_extra:
         @pl.when(core == 0)
@@ -192,15 +255,16 @@
             project(low_extra)
             stage2(low_extra, 1, e_send, s2_recv)
 
-    n_y = plan.full_y
-    for low in range(0, n_y, LANES):
-        high = min(low + LANES, n_y)
-        out_ref[low:high, low:n_y] = lax.dot_general(
-            r_ref[0:high, low:high], r_ref[0:high, low:n_y], (((0,), (0,)), ((), ())),
-            precision=HIGH, preferred_element_type=jnp.float32,
-        )
-        if low:
-            out_ref[low:high, 0:low] = jnp.zeros((high - low, low), jnp.float32)
+    for index, (low, size) in enumerate(plan.chunks):
+        chunk_done(index, low, size)
+
+        @pl.loop(low, low + size)
+        def _(y):
+            project(y)
+
+        stage2(low, size, s2_send, s2_recv)
+        if index == min(2, len(plan.chunks) - 1):
+            square_r()
 
     size = UNIT * UNIT
     to_row = lax.broadcasted_iota(jnp.int32, (size, size), 0)
@@ -209,150 +273,141 @@
 
     pltpu.make_async_copy(gbuf, gbuf, s2_recv).wait()
 
-    @pl.loop(0, n_y // UNIT)
-    def _(group):
-        rows = pl.ds(pl.multiple_of(group * UNIT, UNIT), UNIT)
-        block = gbuf[rows].reshape(size, LANES)
-        turned = jnp.dot(turn, block, preferred_element_type=jnp.float32).astype(jnp.bfloat16)
-        turned = turned.reshape(UNIT, UNIT, LANES)
-        for a in range(UNIT):
-            mbuf[a // 2, rows, (a % 2) * LANES:(a % 2 + 1) * LANES] = turned[a]
+    def turn_groups(group, count):
+        rows = [pl.ds(pl.multiple_of((group + i) * UNIT, UNIT), UNIT) for i in range(count)]
+        blocks = [gbuf[where].reshape(size, LANES) for where in rows]
+        both = blocks[0] if count == 1 else jnp.concatenate(blocks, axis=1)
+        turned = jnp.dot(turn, both, preferred_element_type=jnp.float32).astype(jnp.bfloat16)
+        turned = turned.reshape(UNIT, UNIT, count * LANES)
+        for i in range(count):
+            for a in range(UNIT):
+                mbuf[rows[i], a * LANES:(a + 1) * LANES] = turned[a, :, i * LANES:(i + 1) * LANES]
+
+    groups = n_y // UNIT
+    pl.loop(0, groups // 2)(lambda pair: turn_groups(2 * pair, 2))
+    if groups % 2:
+        turn_groups(groups - 1, 1)
 
     keep = jnp.where(2 * gy + core < units, 1.0, 0.0).astype(jnp.float32)
     for low in range(0, n_y, LANES):
         high = min(low + LANES, n_y)
-        total = jnp.zeros((high - low, n_y - low), jnp.float32)
-        for a in range(UNIT // 2):
-            total = total + lax.dot_general(
-                mbuf[a, low:high, :], mbuf[a, low:n_y, :], (((1,), (1,)), ((), ())),
-                preferred_element_type=jnp.float32,
-            )
-        gram[low:high, low:n_y] = total * keep
-
-    gap = plan.y_lanes - n_y
-    for index, (row, tile) in enumerate(plan.tiles):
-        width = min(LANES, n_y - tile * LANES)
-        if width < LANES:
-            tiles[index] = jnp.zeros((ROWS, LANES), jnp.float32)
-        tiles[index, :, 0:width] = gram[row:row + ROWS, tile * LANES:tile * LANES + width]
-    for index in range(len(plan.tiles), plan.n_tiles):
-        tiles[index] = jnp.zeros((ROWS, LANES), jnp.float32)
-
-    half, piece, own = plan.half, plan.piece, plan.per_owner
-    my_half = core * half
-    other_half = (1 - core) * half
-    send = remote(
-        tiles.at[pl.ds(other_half, half)], core_in, rs_send.at[0], rs_recv.at[0], 2 * xi + 1 - core, gy
-    )
-    send.start()
-    send.wait()
-
-    def add_core(i):
-        tiles[my_half + i] += core_in[i]
-    pl.loop(0, half)(add_core)
-
-    x_sends = []
-    for step in range(1, chips):
-        to = lax.rem(xi + step, chips)
-        send = remote(
-            tiles.at[pl.ds(my_half + to * piece, piece)], x_in.at[step], rs_send.at[1], rs_recv.at[step],
-            2 * to + core, gy,
+        gram[low:high, low:n_y] = keep * lax.dot_general(
+            mbuf[low:high, :], mbuf[low:n_y, :], (((1,), (1,)), ((), ())), preferred_element_type=jnp.float32
         )
-        send.start()
-        x_sends.append(send)
-    for send in x_sends:
-        send.wait_recv()
-    my_piece = my_half + xi * piece
-
-    def add_x(i):
-        value = tiles[my_piece + i]
-        for step in range(1, chips):
-            value = value + x_in[step, i]
-        tiles[my_piece + i] = value
-    pl.loop(0, piece)(add_x)
-
-    @pl.loop(1, n_gy)
-    def _(step):
-        to = lax.rem(gy + step, n_gy)
-
-        @pl.when(to < plan.owners)
-        def _():
-            remote(
-                tiles.at[pl.ds(my_piece + to * own, own)], y_in.at[pl.ds(gy * own, own)], rs_send.at[2], rs_recv.at[chips],
-                gx, to,
-            ).start()
-
-    @pl.when(gy < plan.owners)
-    def _():
-        mine = my_piece + gy * own
-        pltpu.make_async_copy(
-            tiles.at[pl.ds(mine, own)], y_in.at[pl.ds(gy * own, own)], rs_recv.at[chips]
-        ).start()
-        pltpu.make_async_copy(y_in, y_in, rs_recv.at[chips]).wait()
-        for i in range(own):
-            value = y_in[i]
-            for source in range(1, n_gy):
-                value = value + y_in[source * own + i]
-            summed[mine + i] = value
-
-        @pl.loop(1, n_gy)
-        def _(step):
-            to = lax.rem(gy + step, n_gy)
-            remote(
-                summed.at[pl.ds(mine, own)], summed.at[pl.ds(mine, own)], rs_send.at[3], e_recv.at[0], gx, to
-            ).start()
-
-    sent_own = tiles.at[pl.ds(my_piece, own)]
-
-    @pl.loop(1, n_gy)
-    def _(step):
-        to = lax.rem(gy + step, n_gy)
-
-        @pl.when(to < plan.owners)
-        def _():
-            pltpu.make_async_copy(sent_own, sent_own, rs_send.at[2]).wait()
-
-    whole = summed.at[pl.ds(my_piece, piece)]
-    rest = summed.at[pl.ds(my_piece, piece - own)]
-
-    @pl.when(gy < plan.owners)
-    def _():
-        if plan.owners > 1:
-            pltpu.make_async_copy(rest, rest, e_recv.at[0]).wait()
-
-    @pl.when(gy >= plan.owners)
-    def _():
-        pltpu.make_async_copy(whole, whole, e_recv.at[0]).wait()
-
-    gathers = []
-    for step in range(1, chips):
-        to = lax.rem(xi + step, chips)
-        send = remote(whole, whole, rs_send.at[4], e_recv.at[step], 2 * to + core, gy)
-        send.start()
-        gathers.append(send)
-    for send in gathers:
-        send.wait_recv()
-    mine_half = summed.at[pl.ds(my_half, half)]
-    last = remote(mine_half, mine_half, rs_send.at[5], e_recv.at[chips], 2 * xi + 1 - core, gy)
-    last.start()
-    last.wait()
-
-    for index, (row, tile) in enumerate(plan.tiles):
-        width = min(LANES, n_y - tile * LANES)
-        where = (slice(row, row + ROWS), slice(tile * LANES, tile * LANES + width))
-        out_ref[where] = out_ref[where] + summed[index, :, 0:width]
-
-    for send in x_sends:
-        send.wait_send()
-    for send in gathers:
-        send.wait_send()
-
-    @pl.when(gy < plan.owners)
-    def _():
-        @pl.loop(1, n_gy)
-        def _(step):
-            own_tiles = y_in.at[pl.ds(0, own)]
-            pltpu.make_async_copy(own_tiles, own_tiles, rs_send.at[3]).wait()
+
+    @pl.loop(0, plan.n_tiles)
+    def _(i):
+        tiles[i] = jnp.zeros((ROWS, LANES), jnp.float32)
+
+    for row, column, width, tile, lane in plan.pieces:
+        tiles[tile, :, lane:lane + width] = gram[row:row + ROWS, column:column + width]
+
+    own, slots = plan.per_owner, plan.slots
+    yi, zi = gy // plan.n_z, gy % plan.n_z
+    half_low = core * plan.half
+    other_low = (1 - core) * plan.half
+    sibling = 2 * xi + 1 - core
+    started = []
+
+    def send(src, dst, send_sem, recv_sem, to_gx, to_gy):
+        copy = remote(src, dst, send_sem, recv_sem, to_gx, to_gy)
+        copy.start()
+        started.append(copy)
+        return copy
+
+    def along(axis, step):
+        if axis == 0:
+            to = lax.rem(xi + step, chips)
+            return to, 2 * to + core, gy
+        to = lax.rem(yi + step, plan.n_yy)
+        return to, gx, plan.n_z * to + zi
+
+    def span(tile, count):
+        return pl.ds(tile, count)
+
+    places = (xi, yi)
+    counts = (chips, plan.n_yy)
+    send(tiles.at[span(other_low, plan.half)], core_in, rs_send.at[0, 0], rs_recv.at[0, 0], sibling, gy).wait_recv()
+
+    @pl.loop(0, plan.half)
+    def _(i):
+        tiles[half_low + i] = tiles[half_low + i] + core_in[i]
+
+    lows = [half_low, half_low + plan.part]
+    for phase in range(2):
+        waits = []
+        sizes = [plan.part // chips, plan.part // plan.n_yy] if phase == 0 else [slots * own] * 2
+        for part in range(2):
+            axis = part if phase == 0 else 1 - part
+            for step in range(1, counts[axis]):
+                to, to_gx, to_gy = along(axis, step)
+                waits.append(send(
+                    tiles.at[span(lows[part] + to * sizes[part], sizes[part])],
+                    axis_in.at[2 * phase + part, step, span(0, sizes[part])],
+                    rs_send.at[1 + 2 * phase + part, step], rs_recv.at[1 + 2 * phase + part, step], to_gx, to_gy,
+                ))
+        for copy in waits:
+            copy.wait_recv()
+        for part in range(2):
+            axis = part if phase == 0 else 1 - part
+            lows[part] = lows[part] + places[axis] * sizes[part]
+
+            def add(i):
+                value = tiles[lows[part] + i]
+                for step in range(1, counts[axis]):
+                    value = value + axis_in[2 * phase + part, step, i]
+                tiles[lows[part] + i] = value
+            pl.loop(0, sizes[part])(add)
+
+    def slot_tile(z):
+        return jnp.where(z < slots, lows[0] + z * own, lows[1] + (z - slots) * own)
+
+    waits = []
+    for step in range(1, plan.n_z):
+        to = lax.rem(zi + step, plan.n_z)
+        waits.append(send(
+            tiles.at[span(slot_tile(to), own)], z_in.at[step], rs_send.at[5, step], rs_recv.at[5, step],
+            gx, plan.n_z * yi + to,
+        ))
+    for copy in waits:
+        copy.wait_recv()
+    mine = slot_tile(zi)
+    for i in range(own):
+        value = tiles[mine + i]
+        for step in range(1, plan.n_z):
+            value = value + z_in[step, i]
+        summed[mine + i] = value
+
+    waits = []
+    for step in range(1, plan.n_z):
+        to = lax.rem(zi + step, plan.n_z)
+        here = summed.at[span(mine, own)]
+        waits.append(send(here, here, rs_send.at[6, step], rs_recv.at[6, step], gx, plan.n_z * yi + to))
+    for copy in waits:
+        copy.wait_recv()
+    for phase in (1, 0):
+        waits = []
+        for part in range(2):
+            axis = part if phase == 0 else 1 - part
+            count = slots * own if phase == 1 else plan.part // counts[part]
+            low = lows[part] if phase == 1 else half_low + part * plan.part + places[part] * count
+            here = summed.at[span(low, count)]
+            for step in range(1, counts[axis]):
+                _, to_gx, to_gy = along(axis, step)
+                waits.append(send(
+                    here, here, rs_send.at[7 + 2 * phase + part, step], rs_recv.at[7 + 2 * phase + part, step], to_gx, to_gy
+                ))
+        for copy in waits:
+            copy.wait_recv()
+    here = summed.at[span(half_low, plan.half)]
+    send(here, here, rs_send.at[0, 1], rs_recv.at[0, 1], sibling, gy).wait_recv()
+
+    for row, column, width, tile, lane in plan.pieces:
+        where = (slice(row, row + ROWS), slice(column, column + width))
+        out_ref[where] = out_ref[where] + summed[tile, :, lane:lane + width]
+
+    for copy in started:
+        copy.wait_send()
 
     for index, (low, size) in enumerate(plan.chunks):
         there = fbuf.at[pl.ds(low, size), 0]
@@ -387,43 +442,45 @@
 
 def updated_total(plan, fields, x_factor, running_r):
     by_y = jnp.transpose(fields, (1, 0, 2))
-    xt = jnp.transpose(x_factor).reshape(plan.rank, plan.n_gx, plan.x_block)
-    xt = jnp.pad(xt, ((0, 0), (0, 0), (0, plan.x_pad - plan.x_block))).reshape(plan.rank, plan.n_gx * plan.x_pad)
     n_y = plan.full_y
     chunks = len(plan.chunks) + 1
     vmem = pl.BlockSpec(memory_space=pltpu.VMEM)
     return pl.pallas_call(
         functools.partial(exchange_kernel, plan),
         out_shape=jax.ShapeDtypeStruct((n_y, n_y), jnp.float32),
-        in_specs=[pl.BlockSpec(memory_space=pl.ANY), vmem, vmem],
+        in_specs=[pl.BlockSpec(memory_space=pl.ANY)] * 3,
         out_specs=vmem,
         scratch_shapes=[
             pltpu.VMEM((plan.y_first, plan.n_gx, plan.x_block, plan.part_cells), jnp.bfloat16),
             pltpu.VMEM((plan.n_gx * plan.x_pad, plan.part_cells), jnp.bfloat16),
+            pltpu.VMEM(x_factor.shape, jnp.bfloat16),
+            pltpu.VMEM((plan.n_gx * plan.x_pad, plan.rank), jnp.bfloat16),
+            pltpu.VMEM((plan.rank, plan.n_gx * plan.x_pad), jnp.bfloat16),
+            pltpu.VMEM((n_y, n_y), jnp.float32),
             pltpu.VMEM((plan.y_first, plan.units, UNIT, LANES), jnp.bfloat16),
             pltpu.VMEM((n_y, UNIT, LANES), jnp.bfloat16),
-            pltpu.VMEM((UNIT // 2, n_y, 2 * LANES), jnp.bfloat16),
+            pltpu.VMEM((n_y, UNIT * LANES), jnp.bfloat16),
             pltpu.VMEM((n_y, n_y), jnp.float32),
             pltpu.VMEM((plan.n_tiles, ROWS, LANES), jnp.float32),
             pltpu.VMEM((plan.n_tiles, ROWS, LANES), jnp.float32),
             pltpu.VMEM((plan.half, ROWS, LANES), jnp.float32),
-            pltpu.VMEM((plan.chips, plan.piece, ROWS, LANES), jnp.float32),
-            pltpu.VMEM((plan.n_gy * plan.per_owner, ROWS, LANES), jnp.float32),
+            pltpu.VMEM((4, max(plan.chips, plan.n_yy), plan.part // min(plan.chips, plan.n_yy), ROWS, LANES), jnp.float32),
+            pltpu.VMEM((plan.n_z, plan.per_owner, ROWS, LANES), jnp.float32),
             pltpu.SemaphoreType.DMA((chunks,)),
             pltpu.SemaphoreType.DMA((chunks, plan.n_gx)),
             pltpu.SemaphoreType.DMA,
             pltpu.SemaphoreType.DMA,
             pltpu.SemaphoreType.DMA,
-            pltpu.SemaphoreType.DMA((plan.chips + 1,)),
-            pltpu.SemaphoreType.DMA((6,)),
-            pltpu.SemaphoreType.DMA((plan.chips + 1,)),
-            pltpu.SemaphoreType.DMA,
+            pltpu.SemaphoreType.DMA((11, 8)),
+            pltpu.SemaphoreType.DMA((11, 8)),
+            pltpu.SemaphoreType.DMA((2,)),
+            pltpu.SemaphoreType.REGULAR((8,)),
         ],
         compiler_params=pltpu.CompilerParams(
-            collective_id=0, has_side_effects=True, vmem_limit_bytes=48 * 1024 * 1024
+            collective_id=0, has_side_effects=True, vmem_limit_bytes=60 * 1024 * 1024
         ),
         name="exchange",
-    )(by_y, xt, running_r)
+    )(by_y, x_factor, running_r)
 
 
 def element(row, lane):

time: 183 us -> 175 us (0.956)
  Pallas kernels: 181 us -> 172 us
    pallas_call x1, Pallas kernels: 144 us -> 136 us  [updated_total(): pl.pallas_call(functools.partial(exchange_kernel, plan), out_shape=jax.Sh...]
where the time goes in v1:
time: 175 us
  Pallas kernels  172 us (98%)
  local copies, waits for them, and re-layouts  2.26 us (1%)
    pallas_call x1, Pallas kernels, updated_total(): pl.pallas_call(functools.partial(exchange_kernel, plan), out_shape=jax.Sh...  136 us
    pallas_call x1, Pallas kernels, upper_factor(): pl.pallas_call(functools.partial(chol_kernel, n), out_shape=jax.ShapeDtyp...  36.6 us

profile of v1, /device:TPU:1, one launch (start us, length us, event | category | flops | bytes accessed | tf_op | source)
XLA Modules:
  0.0 174.7 jit_solution(6776791624000337204)
XLA Ops:
  0.0 135.9 %exchange.1.a_ref = f32[672,672]{1,0:T(8,128)} custom-call(bf16[21,84,1536]{2,1,0:T(8,128)(2,1)} %bitcast.1, bf16[672,336]{1,0:T(8,128)(2,1)} %x_hbm.1, f32[672,672]{1,0:T(8,128)} %r_hbm.1), custom_call_target="tpu_custom_call" | custom-call | tf_op jit(solution)/shard_map/exchange/pallas_call | solution.py:448
  135.9 0.0 copy-start
  135.9 1.6 copy-done
  137.4 36.6 %factor.1 = f32[672,672]{1,0:T(8,128)S(1)} custom-call(f32[672,672]{1,0:T(8,128)S(1)} %copy-done), custom_call_target="tpu_custom_call" | custom-call | tf_op jit(solution)/shard_map/factor/pallas_call | solution.py:585
  174.0 0.7 dynamic_slice.3
Async XLA Ops:
  135.9 1.6 copy-start

commit v2 on v1

--- a/solution.py
+++ b/solution.py
@@ -77,7 +77,7 @@
         sizes = []
         left = self.y_common
         while left:
-            size = 1 if len(sizes) < 2 else 2
+            size = 1
             sizes.append(min(size, left))
             left -= sizes[-1]
         chunks, low = [], 0
@@ -501,7 +501,7 @@
             rows[i] = rows[i] - scaled[i] * top
     return done
 
-def chol_kernel(n, a_ref, u_ref, work, rowbuf, spread):
+def chol_kernel(n, a_ref, u_ref, work, rowbuf, spread, upper):
     nb = -(-n // LANES); width = nb * LANES
     for t in range(nb):
         w = min(LANES, n - t * LANES)
@@ -517,6 +517,9 @@
             return rowbuf[i * ROWS:(i + 1) * ROWS, :]
         def put(i, v):
             rowbuf[i * ROWS:(i + 1) * ROWS, :] = v
+        half = panels // 2 if panels > 8 else panels
+        def rest_end(p):
+            return (half if p < half else panels) * ROWS
         rows = [get(i) for i in range(ROWS)]
         for p in range(panels):
             lane = p * ROWS
@@ -525,17 +528,32 @@
                 put(lane + k, done[k])
             if p + 1 == panels:
                 break
+            if p + 1 == half:
+                for q in range(half):
+                    for s in range(tiles):
+                        upper[s, q * ROWS:(q + 1) * ROWS, :] = rowbuf[pl.ds(q * 64 + s, ROWS, stride=ROWS), :]
+                left = upper[0, :, half * ROWS:]
+                for s in range(tiles):
+                    change = lax.dot_general(left, upper[s], (((0,), (0,)), ((), ())), precision=HIGH, preferred_element_type=jnp.float32)
+                    for q in range(half):
+                        where = pl.ds((half + q) * 64 + s, ROWS, stride=ROWS)
+                        rowbuf[where, :] = rowbuf[where, :] - change[q * ROWS:(q + 1) * ROWS, :]
+                rows = [get(half * ROWS + i) for i in range(ROWS)]
+                continue
             rows = []
+            flat = rowbuf[pl.ds(lane * ROWS, ROWS, stride=ROWS), :]
+            for i in range(ROWS):
+                j = lane + ROWS + i
+                spread[j * ROWS:(j + 1) * ROWS, :] = jnp.broadcast_to(flat[:, j:j + 1], (ROWS, LANES))
             for i in range(ROWS):
                 value = get(lane + ROWS + i)
                 acc = None
                 for k in range(ROWS):
-                    term = element(done[k], lane + ROWS + i) * done[k]
+                    term = spread[pl.ds((lane + ROWS + i) * ROWS + k, ROWS, stride=0), :] * done[k]
                     acc = term if acc is None else acc + term
                 rows.append(value - acc)
-            if p + 2 < panels:
-                flat = rowbuf[pl.ds(lane * ROWS, ROWS, stride=ROWS), :]
-                for i in range((p + 2) * ROWS, panels * ROWS):
+            if (p + 2) * ROWS < rest_end(p):
+                for i in range((p + 2) * ROWS, rest_end(p)):
                     spread[i * ROWS:(i + 1) * ROWS, :] = jnp.broadcast_to(flat[:, i:i + 1], (ROWS, LANES))
                     acc = None
                     for k in range(ROWS):
@@ -586,7 +604,7 @@
         functools.partial(chol_kernel, n),
         out_shape=jax.ShapeDtypeStruct((n, n), jnp.float32),
         in_specs=[pl.BlockSpec(memory_space=pltpu.VMEM)], out_specs=pl.BlockSpec(memory_space=pltpu.VMEM),
-        scratch_shapes=[pltpu.VMEM((nb, nb * LANES, LANES), jnp.float32), pltpu.VMEM((LANES * ROWS, LANES), jnp.float32), pltpu.VMEM((LANES * ROWS, LANES), jnp.float32)],
+        scratch_shapes=[pltpu.VMEM((nb, nb * LANES, LANES), jnp.float32), pltpu.VMEM((LANES * ROWS, LANES), jnp.float32), pltpu.VMEM((LANES * ROWS, LANES), jnp.float32), pltpu.VMEM((nb, LANES // 2, LANES), jnp.float32)],
         compiler_params=pltpu.CompilerParams(vmem_limit_bytes=40 * 1024 * 1024), name="factor",
     )(a)
 

time: 175 us -> 169 us (0.966)
  Pallas kernels: 172 us -> 166 us
    pallas_call x1, Pallas kernels: 36.6 us -> 31.5 us  [upper_factor(): pl.pallas_call(functools.partial(chol_kernel, n), out_shape=jax.ShapeDtyp...]
where the time goes in v2:
time: 169 us
  Pallas kernels  166 us (98%)
  local copies, waits for them, and re-layouts  2.26 us (1%)
    pallas_call x1, Pallas kernels, updated_total(): pl.pallas_call(functools.partial(exchange_kernel, plan), out_shape=jax.Sh...  135 us
    pallas_call x1, Pallas kernels, upper_factor(): pl.pallas_call(functools.partial(chol_kernel, n), out_shape=jax.ShapeDtyp...  31.5 us

profile of v2, /device:TPU:1, one launch (start us, length us, event | category | flops | bytes accessed | tf_op | source)
XLA Modules:
  0.0 168.6 jit_solution(16169622254730940257)
XLA Ops:
  0.0 134.8 %exchange.1.a_ref = f32[672,672]{1,0:T(8,128)} custom-call(bf16[21,84,1536]{2,1,0:T(8,128)(2,1)} %bitcast.1, bf16[672,336]{1,0:T(8,128)(2,1)} %x_hbm.1, f32[672,672]{1,0:T(8,128)} %r_hbm.1), custom_call_target="tpu_custom_call" | custom-call | tf_op jit(solution)/shard_map/exchange/pallas_call | solution.py:448
  134.8 0.0 copy-start
  134.8 1.6 copy-done
  136.4 31.5 %factor.1 = f32[672,672]{1,0:T(8,128)S(1)} custom-call(f32[672,672]{1,0:T(8,128)S(1)} %copy-done), custom_call_target="tpu_custom_call" | custom-call | tf_op jit(solution)/shard_map/factor/pallas_call | solution.py:603
  167.9 0.7 dynamic_slice.3
Async XLA Ops:
  134.8 1.6 copy-start
